TPU v7x, 32 devices: a whole 2x2x4 slice. The times are simulated.
32 devices in a mesh: samp: 1, vert: 32 (over z, y, x, core).
Axes of the slice: x: 2, y: 2, z: 4, core: 2. Of those that a mesh axis runs over, the one named last changes fastest.
Arguments:
- inputs: bfloat16 [2, 131072, 128], P('samp', 'vert'), may hold values from -6 to 6
- cotangent: bfloat16 [2, 131072, 128], P('samp', 'vert'), may hold values from -6 to 6
- basis: bfloat16 [131072, 1024], P('vert'), may hold values from -0.03125 to 0.03125
- mode_weights: bfloat16 [1024, 128, 128], P('vert'), may hold values from -0.5 to 0.5
- w_up: bfloat16 [128, 512], replicated, may hold values from -0.5 to 0.5
- b_up: float32 [512], replicated, may hold values from -4 to 4
- w_down: bfloat16 [512, 128], replicated, may hold values from -0.25 to 0.25
Outputs:
- grad_input: bfloat16 [2, 131072, 128], P('samp', 'vert')
- grad_modes: float32 [1024, 128, 128], P('vert')
- grad_w_up: float32 [128, 512], replicated
- grad_b_up: float32 [512], replicated
- grad_w_down: float32 [512, 128], replicated
All inputs are finite; a program needn't handle non-finite values.
Results may differ from a plain program's by a relative error of at most 0.0055.
Values may be sent and summed in bfloat16 or wider, within the bound.
A program may use at most 128 MiB of HBM per device.

v0:
```python
import jax
import jax.numpy as jnp
from jax import lax
from jax.sharding import PartitionSpec as P


def gelu_value(pre_act):
    inner = 0.7978845608 * (pre_act + 0.044715 * pre_act * pre_act * pre_act)
    return 0.5 * pre_act * (1.0 + jnp.tanh(inner))


def gelu_slope(pre_act):
    inner = 0.7978845608 * (pre_act + 0.044715 * pre_act * pre_act * pre_act)
    tangent = jnp.tanh(inner)
    return 0.5 * (1.0 + tangent) + 0.5 * pre_act * (1.0 - tangent * tangent) * 0.7978845608 * (
        1.0 + 3.0 * 0.044715 * pre_act * pre_act
    )


def spectral_part(grad_out, mode_weights, basis):
    mixing = mode_weights.astype(jnp.float32)
    grad_coef = jnp.einsum(
        "skd,kcd->skc", grad_out, mixing, precision=lax.Precision.HIGHEST
    ).astype(jnp.bfloat16)
    return jnp.einsum(
        "vk,skc->svc",
        basis,
        lax.all_gather(grad_coef, "vert", axis=1, tiled=True),
        preferred_element_type=jnp.float32,
    )


def pointwise_part(inputs, cotangent, w_up, b_up, w_down):
    samples_here = inputs.shape[0]
    vertices_here = inputs.shape[1]
    channels = inputs.shape[2]
    flat_inputs = inputs.reshape(samples_here * vertices_here, channels)
    flat_cotangent = cotangent.reshape(samples_here * vertices_here, channels)
    pre_act = jnp.dot(flat_inputs, w_up, preferred_element_type=jnp.float32) + b_up
    hidden = gelu_value(pre_act).astype(jnp.bfloat16)
    grad_hidden = jnp.dot(flat_cotangent, w_down.T, preferred_element_type=jnp.float32)
    grad_pre = (grad_hidden * gelu_slope(pre_act)).astype(jnp.bfloat16)
    pointwise = jnp.dot(grad_pre, w_up.T, preferred_element_type=jnp.float32)
    local_up = jnp.dot(flat_inputs.T, grad_pre, preferred_element_type=jnp.float32)
    local_bias = jnp.sum(grad_pre.astype(jnp.float32), axis=0)
    local_down = jnp.dot(hidden.T, flat_cotangent, preferred_element_type=jnp.float32)
    sums = lax.psum((local_up, local_bias, local_down), ("samp", "vert"))
    return (pointwise.reshape(samples_here, vertices_here, channels), sums)


def per_device(inputs, cotangent, basis, mode_weights, w_up, b_up, w_down):
    channels = inputs.shape[2]
    stacked = jnp.concatenate([inputs, cotangent], axis=2)
    projected = jnp.einsum("vk,svc->skc", basis, stacked, preferred_element_type=jnp.float32)
    owned_sums = lax.psum_scatter(projected, "vert", scatter_dimension=1, tiled=True)
    coeffs = owned_sums[:, :, :channels]
    grad_out = owned_sums[:, :, channels:]
    spectral = spectral_part(grad_out, mode_weights, basis)
    pointwise, mlp_grads = pointwise_part(inputs, cotangent, w_up, b_up, w_down)
    local_modes = jnp.einsum("skc,skd->kcd", coeffs, grad_out, precision=lax.Precision.HIGHEST)
    grad_modes = lax.psum(local_modes, "samp")
    grad_input = (spectral + pointwise).astype(jnp.bfloat16)
    grad_w_up, grad_b_up, grad_w_down = mlp_grads
    return (grad_input, grad_modes, grad_w_up, grad_b_up, grad_w_down)


def solution(mesh):
    in_specs = (
        P("samp", "vert", None),
        P("samp", "vert", None),
        P("vert", None),
        P("vert", None, None),
        P(),
        P(),
        P(),
    )
    out_specs = (P("samp", "vert", None), P("vert", None, None), P(), P(), P())
    return jax.shard_map(
        per_device, mesh=mesh, in_specs=in_specs, out_specs=out_specs, check_vma=False
    )
```

profile of v0, /device:TPU:0, one launch (start us, length us, event | category | flops | bytes accessed | tf_op | source)
XLA Modules:
  0.0 264.8 jit_solution(16600120702481336750)
XLA Ops:
  7.2 0.0 copy-start
  7.2 0.0 copy-start.1
  7.2 0.0 copy-start.5
  7.2 0.0 all-reduce.4.cloned.1.call-start
  7.2 4.2 %copy.32 = bf16[2,4096,128]{1,2,0:T(8,128)(2,1)} copy(bf16[2,4096,128]{2,1,0:T(8,128)(2,1)} %param.7) | data formatting | bytes 4194304 | tf_op args[0]
  11.5 4.1 %copy.33 = bf16[2,4096,128]{1,2,0:T(8,128)(2,1)} copy(bf16[2,4096,128]{2,1,0:T(8,128)(2,1)} %param.8) | data formatting | bytes 4194304 | tf_op args[1]
  15.6 0.0 copy-done.1
  15.6 0.0 copy-done.5
  15.6 0.0 copy-start.2
  15.6 0.0 copy-start.8
  15.6 2.3 fusion.42
  17.9 0.0 copy-done.2
  17.9 0.0 copy-done.8
  17.9 0.0 copy-start.7
  17.9 7.7 %fusion.11 = f32[512,128]{1,0:T(8,128)} fusion(bf16[8192,128]{1,0:T(8,128)(2,1)S(1)} %bitcast.42, f32[8192,512]{1,0:T(8,128)S(1)} %fusion.42, f32[512]{0:T(512)S(1)} %copy-done.8), kind=kOutput, calls=%fused_computation.15 | convolution fusion | flops 1115684864 | bytes 19138560 | tf_op jit(solution)/shard_map/dot_general | solution.py:46
  25.7 0.0 copy-done.7
  25.7 14.9 %convert_reduce_fusion = (f32[512]{0:T(512)S(1)}, bf16[8192,512]{1,0:T(8,128)(2,1)}) fusion(f32[8192,512]{1,0:T(8,128)S(1)} %fusion.42, f32[512]{0:T(512)S(1)} %copy-done.8, bf16[8192,128]{1,0:T(8,128)(2,1)} %bitcast.41, bf16[512,128]{1,0:T(8,128)(2,1)S(1)} %copy-done.7), kind=kOutput, calls=%fused_computation.10 | convolution fusion | flops 1166016000 | bytes 27398144 | tf_op jit(solution)/shard_map/dot_general | solution.py:41
  40.5 0.0 copy-start.3
  40.5 0.0 copy-start.4
  40.5 6.6 %convolution_bitcast_fusion = f32[128,512]{0,1:T(8,128)} fusion(bf16[8192,512]{1,0:T(8,128)(2,1)} %get-tuple-element.29, bf16[8192,128]{1,0:T(8,128)(2,1)S(1)} %bitcast.40), kind=kOutput, calls=%fused_computation.23 | convolution fusion | flops 1073741824 | bytes 10747904 | tf_op jit(solution)/shard_map/dot_general | solution.py:44
  47.1 0.0 copy-done.3
  47.1 0.0 copy-done.4
  47.1 6.9 %fusion.24 = f32[2,1024,256]{1,2,0:T(8,128)S(1)} fusion(bf16[4096,1024]{1,0:T(8,128)(2,1)} %param.9, bf16[2,4096,128]{1,2,0:T(8,128)(2,1)S(1)} %copy-done.4, bf16[2,4096,128]{1,2,0:T(8,128)(2,1)S(1)} %copy-done.3), kind=kOutput, calls=%fused_computation.22 | convolution fusion | flops 4303355904 | bytes 14680064 | tf_op jit(solution)/shard_map/vk,svc->skc/dot_general | solution.py:54
  54.0 2.3 copy.34
  56.3 0.0 all-reduce.4.cloned.1.call-update
  56.4 7.7 %fusion.43 = f32[8192,128]{1,0:T(8,128)} fusion(bf16[8192,512]{1,0:T(8,128)(2,1)} %get-tuple-element.29, bf16[128,512]{1,0:T(8,128)(2,1)S(1)} %copy-done.5), kind=kOutput, calls=%fused_computation.39 | convolution fusion | flops 1073741824 | bytes 12713984 | tf_op jit(solution)/shard_map/dot_general | solution.py:43
  64.1 5.8 %copy.36 = f32[2,4096,128]{1,2,0:T(8,128)} copy(f32[2,4096,128]{2,1,0:T(8,128)} %bitcast.38) | data formatting | bytes 8388608 | tf_op jit(solution)/shard_map/reshape | solution.py:48
  69.9 41.7 %psum.25 = f32[512]{0:T(512)} all-reduce(f32[512]{0:T(512)S(1)} %get-tuple-element.28), channel_id=1, replica_groups=mesh['samp'=1,'vert'=32] {'samp','vert'}, use_global_device_ids=true, to_apply=%region_3.0 | all-reduce | flops 512 | bytes 4096 | tf_op jit(solution)/shard_map/psum | solution.py:47
  111.6 84.9 %all-reduce.4.cloned.1.call-done = (f32[2,1024,256]{2,0,1:T(2,128)}, f32[128,512]{0,1:T(8,128)}, f32[512,128]{1,0:T(8,128)}) async-done(((f32[2,1024,256]{2,0,1:T(2,128)}, f32[128,512]{0,1:T(8,128)}, f32[512,128]{1,0:T(8,128)}), (f32[2,1024,256]{2,0,1:T(2,128)}, f32[128,512]{0,1:T(8,128)}, f32[512,128]{1,0:T(8,128)})) %all-reduce.4.cloned.1.call-update) | async-done | bytes 2621456
  196.5 5.6 %fusion.31 = f32[32,128,128]{2,1,0:T(8,128)} fusion(f32[2,1024,256]{2,0,1:T(2,128)} %get-tuple-element.25, u32[]{:T(128)S(6)} %multiply.1, u32[]{:T(128)S(6)} %convert), kind=kOutput, calls=%fused_computation.27 | convolution fusion | flops 12582912 | bytes 2164224 | tf_op jit(solution)/shard_map/skc,skd->kcd/dot_general | solution.py:60
  202.1 0.0 copy-done
  202.1 2.5 fusion.29
  204.6 41.4 %all_gather.3 = bf16[2,1024,128]{2,0,1:T(2,128)(2,1)S(1)} all-gather(bf16[2,32,128]{2,0,1:T(2,128)(2,1)S(1)} %fusion.29), channel_id=1, replica_groups=mesh['samp'=1,'vert'=32] {'vert'}, dimensions={1}, use_global_device_ids=true | all-gather | bytes 540672 | tf_op jit(solution)/shard_map/all_gather | solution.py:28
  246.0 0.0 copy-start.6
  246.0 7.0 %fusion.18 = bf16[2,4096,128]{1,2,0:T(8,128)(2,1)S(1)} fusion(f32[2,4096,128]{1,2,0:T(8,128)} %copy.36, bf16[4096,1024]{1,0:T(8,128)(2,1)} %param.9, bf16[2,1024,128]{2,0,1:T(2,128)(2,1)S(1)} %all_gather.3), kind=kOutput, calls=%fused_computation.18 | convolution fusion | flops 2149580800 | bytes 15204352 | tf_op jit(solution)/shard_map/vk,skc->svc/dot_general | solution.py:25
  253.0 2.5 copy.37
  255.4 1.8 copy.38
  257.2 0.0 copy-done.6
  257.2 0.7 copy.44
Async XLA Ops:
  7.2 194.9 %copy-start = (bf16[32,128,128]{2,1,0:T(8,128)(2,1)S(1)}, bf16[32,128,128]{2,1,0:T(8,128)(2,1)}, u32[]{:S(2)}) copy-start(bf16[32,128,128]{2,1,0:T(8,128)(2,1)} %param.10) | copy-start | bytes 3145732
  7.2 8.4 %copy-start.1 = (bf16[2,4096,128]{2,1,0:T(8,128)(2,1)S(1)}, bf16[2,4096,128]{2,1,0:T(8,128)(2,1)}, u32[]{:S(2)}) copy-start(bf16[2,4096,128]{2,1,0:T(8,128)(2,1)} %param.7) | copy-start | bytes 6291460
  7.2 8.4 %copy-start.5 = (bf16[128,512]{1,0:T(8,128)(2,1)S(1)}, bf16[128,512]{1,0:T(8,128)(2,1)}, u32[]{:S(2)}) copy-start(bf16[128,512]{1,0:T(8,128)(2,1)} %param.11) | copy-start | bytes 393220
  7.2 189.3 %all-reduce.4.cloned.1.call-start = ((), (), s32[]{:S(2)}) async-start(), calls=%async_computation | async-start | bytes 5242880
  15.6 2.4 copy-start.2
  15.6 2.4 copy-start.8
  17.9 7.7 %copy-start.7 = (bf16[512,128]{1,0:T(8,128)(2,1)S(1)}, bf16[512,128]{1,0:T(8,128)(2,1)}, u32[]{:S(2)}) copy-start(bf16[512,128]{1,0:T(8,128)(2,1)} %param.13) | copy-start | bytes 393220
  40.5 6.6 %copy-start.3 = (bf16[2,4096,128]{1,2,0:T(8,128)(2,1)S(1)}, bf16[2,4096,128]{1,2,0:T(8,128)(2,1)}, u32[]{:S(2)}) copy-start(bf16[2,4096,128]{1,2,0:T(8,128)(2,1)} %copy.32) | copy-start | bytes 6291460
  40.5 6.6 %copy-start.4 = (bf16[2,4096,128]{1,2,0:T(8,128)(2,1)S(1)}, bf16[2,4096,128]{1,2,0:T(8,128)(2,1)}, u32[]{:S(2)}) copy-start(bf16[2,4096,128]{1,2,0:T(8,128)(2,1)} %copy.33) | copy-start | bytes 6291460
  246.0 11.3 %copy-start.6 = (f32[512,128]{1,0:T(8,128)S(1)}, f32[512,128]{1,0:T(8,128)}, u32[]{:S(2)}) copy-start(f32[512,128]{1,0:T(8,128)} %get-tuple-element.34) | copy-start | bytes 786436
Sparse Core Ops, SparseCore 0:
  56.5 139.9 all-reduce.3
where the time goes:
time: 265 us
  waiting for transfers between devices  84.9 us (32%)
  blocking collectives  83 us (31%)
  matrix products  61.2 us (23%)
  local copies, waits for them, and re-layouts  21.5 us (8%)
  between operations  14.1 us (5%)
    unnamed x2, waiting for transfers between devices  84.9 us
    psum x1, blocking collectives, pointwise_part(): sums = lax.psum((local_up, local_bias, local_down), ('samp', 'vert'))  41.7 us
    all_gather x1, blocking collectives, spectral_part(): lax.all_gather(grad_coef, 'vert', axis=1, tiled=True)  41.4 us
    dot_general x1, matrix products, pointwise_part(): jnp.dot(flat_cotangent, w_down.T, preferred_element_type=jnp.float32)  14.9 us
    unnamed x23, local copies, waits for them, and re-layouts  13.3 us
    dot_general x1, matrix products, pointwise_part(): jnp.dot(hidden.T, flat_cotangent, preferred_element_type=jnp.float32)  7.72 us
    dot_general x1, matrix products, pointwise_part(): pointwise = jnp.dot(grad_pre, w_up.T, preferred_element_type=jnp.float32)  7.69 us
    dot_general x1, matrix products, spectral_part(): jnp.einsum('vk,skc->svc', basis, lax.all_gather(grad_coef, 'vert', axis=1...  7.03 us
  transfers between devices with their start and end apart: 1, of which 1 were waited for; matrix products, arithmetic and copies ran while one was open for 5% of the time, Pallas kernels for 0%

commit v1 on v0

v1 whole, which is shorter than its diff:
```python
import functools

import jax
import jax.numpy as jnp
from jax import lax
from jax.experimental import pallas as pl
from jax.experimental.pallas import tpu as pltpu
from jax.sharding import PartitionSpec as P

F32 = jnp.float32
BF16 = jnp.bfloat16
MESH = pl.DeviceIdType.MESH
ROOT = 0.7978845608
CUBE = 0.044715


def radices_of(size):
    radices = []
    if size % 4 == 0:
        radices.append(4)
        size //= 4
    while size > 1:
        step = 2 if size % 2 == 0 else size
        radices.append(step)
        size //= step
    return tuple(radices) or (1,)


def dot(left, right, contract):
    return lax.dot_general(left, right, (contract, ((), ())), preferred_element_type=F32)


def layer_kernel(
    plan,
    inputs_hbm, cotangent_hbm, basis_hbm, modes_hbm, w_up, b_up, w_down,
    grad_input_hbm, grad_modes_hbm, grad_up, grad_bias, grad_down,
    xs, cs, xt, basis, modes, acc, pointwise, result, outer,
    up_acc, down_acc, bias_acc, gathered, natural, left_rows, right_rows, mixed,
    weights_all, in_sems, out_sems, send_sems, recv_sems, *stages,
):
    size, radices = plan["size"], plan["radices"]
    samples, here, chan = xs.shape
    hidden_units = w_up.shape[1]
    total_modes = basis.shape[1]
    owned = total_modes // size
    depth = len(radices)
    coef_f32 = stages[0:depth]
    coef_send = stages[depth:2 * depth]
    coef_recv = stages[2 * depth:3 * depth]
    weight_f32 = stages[3 * depth:4 * depth]
    weight_recv = stages[4 * depth:5 * depth]
    bias_slots = stages[5 * depth:6 * depth]

    me = lax.axis_index("vert")
    strides = [1] * depth
    for at in range(depth - 2, -1, -1):
        strides[at] = strides[at + 1] * radices[at + 1]
    digits = [lax.rem(lax.div(me, strides[at]), radices[at]) for at in range(depth)]

    def peer(at, shift):
        digit = lax.rem(digits[at] + shift, radices[at])
        return digit, {"vert": me + (digit - digits[at]) * strides[at]}

    load_steps = plan["load_steps"]
    load_rows = here // load_steps

    def loads(step):
        rows = pl.ds(pl.multiple_of(step * load_rows, load_rows), load_rows)
        return (
            pltpu.make_async_copy(inputs_hbm.at[:, rows], xs.at[:, rows], in_sems.at[0, step]),
            pltpu.make_async_copy(cotangent_hbm.at[:, rows], cs.at[:, rows], in_sems.at[1, step]),
            pltpu.make_async_copy(basis_hbm.at[rows], basis.at[rows], in_sems.at[2, step]),
        )

    for step in range(load_steps):
        for copy in loads(step):
            copy.start()
    modes_copy = pltpu.make_async_copy(modes_hbm, modes, in_sems.at[3, 0])
    modes_copy.start()

    barrier = pltpu.get_barrier_semaphore()
    peers = 0
    for at in range(depth):
        for shift in range(1, radices[at]):
            pl.semaphore_signal(barrier, inc=1, device_id=peer(at, shift)[1], device_id_type=MESH)
            peers += 1

    acc[...] = jnp.zeros_like(acc)
    up_acc[...] = jnp.zeros_like(up_acc)
    down_acc[...] = jnp.zeros_like(down_acc)
    bias_acc[...] = jnp.zeros_like(bias_acc)

    def project(step, carry):
        for copy in loads(step):
            copy.wait()
        rows = pl.ds(pl.multiple_of(step * load_rows, load_rows), load_rows)
        for s in range(samples):
            xt[2 * s * chan:(2 * s + 1) * chan, rows] = xs[s, rows, :].T
            xt[(2 * s + 1) * chan:(2 * s + 2) * chan, rows] = cs[s, rows, :].T
        acc[...] += dot(xt[:, rows], basis[rows, :], ((1,), (0,)))
        return carry

    lax.fori_loop(0, load_steps, project, 0)

    first = radices[-1]
    for block in range(total_modes // 128):
        tile = acc[:, block * 128:(block + 1) * 128].T
        for part in range(128 // owned):
            owner = block * (128 // owned) + part
            rows = tile[part * owned:(part + 1) * owned]
            coef_f32[0][owner % first, owner // first] = rows
            coef_send[0][owner % first, owner // first] = rows.astype(BF16)

    pl.semaphore_wait(barrier, peers)

    sem_at = [0]

    def exchange(at, pairs):
        copies = []
        for shift in range(1, radices[at]):
            digit, target = peer(at, shift)
            for source_of, dest in pairs:
                copies.append(pltpu.make_async_remote_copy(
                    src_ref=source_of(digit),
                    dst_ref=dest,
                    send_sem=send_sems.at[sem_at[0]],
                    recv_sem=recv_sems.at[sem_at[0]],
                    device_id=target,
                    device_id_type=MESH,
                ))
                sem_at[0] += 1
        for copy in copies:
            copy.start()
        return copies

    def finish(copies):
        for copy in copies:
            copy.wait()

    def scatter_start(turn):
        at = depth - 1 - turn
        return exchange(at, [(lambda digit: coef_send[turn].at[digit], coef_recv[turn].at[digits[at]])])

    def scatter_sum(turn, copies):
        at = depth - 1 - turn
        finish(copies)
        blocks = coef_f32[turn].shape[1]
        sums = []
        for block in range(blocks):
            value = coef_f32[turn][digits[at], block]
            for shift in range(1, radices[at]):
                value = value + coef_recv[turn][peer(at, shift)[0], block].astype(F32)
            if turn + 1 < depth:
                radix = radices[at - 1]
                coef_f32[turn + 1][block % radix, block // radix] = value
                coef_send[turn + 1][block % radix, block // radix] = value.astype(BF16)
            else:
                sums.append(value)
        return sums

    def weights_start(turn):
        at = depth - 1 - turn
        pairs = [
            (lambda digit: weight_f32[turn].at[digit], weight_recv[turn].at[digits[at]]),
            (lambda digit: bias_slots[turn].at[digits[at]], bias_slots[turn].at[digits[at]]),
        ]
        return exchange(at, pairs)

    def weights_sum(turn, copies):
        at = depth - 1 - turn
        finish(copies)
        blocks = weight_f32[turn].shape[1]
        for block in range(blocks):
            value = weight_f32[turn][digits[at], block]
            for shift in range(1, radices[at]):
                value = value + weight_recv[turn][peer(at, shift)[0], block]
            if turn + 1 < depth:
                radix = radices[at - 1]
                weight_f32[turn + 1][block % radix, block // radix] = value
            else:
                weights_all[tuple(reversed(digits))] = value
        bias = bias_slots[turn][0]
        for slot in range(1, radices[at]):
            bias = bias + bias_slots[turn][slot]
        if turn + 1 < depth:
            bias_slots[turn + 1][digits[at - 1]] = bias
        else:
            grad_bias[...] = jnp.sum(bias, axis=0, keepdims=True)

    def gather_start(turn, ref):
        held = ref.at[tuple(reversed(digits[turn:]))]
        return exchange(turn, [(lambda digit: held, held)])

    chunk = plan["chunk"]
    chunks = here // chunk

    def point(step, carry):
        rows = pl.ds(pl.multiple_of(step * chunk, chunk), chunk)
        for s in range(samples):
            z = dot(xs[s, rows, :], w_up[...], ((1,), (0,))) + b_up[...]
            square = z * z
            t = jnp.tanh(z * (ROOT + (ROOT * CUBE) * square))
            half = 0.5 * z
            plus = 1.0 + t
            hidden = (half * plus).astype(BF16)
            slope = plus * (0.5 + half * (1.0 - t) * (ROOT + (3.0 * ROOT * CUBE) * square))
            grad_hidden = dot(cs[s, rows, :], w_down[...], ((1,), (1,)))
            grad_pre = (grad_hidden * slope).astype(BF16)
            pointwise[s, rows, :] = dot(grad_pre, w_up[...], ((1,), (1,)))
            up_acc[...] += dot(xt[2 * s * chan:(2 * s + 1) * chan, rows], grad_pre, ((1,), (0,)))
            down_acc[...] += dot(xt[(2 * s + 1) * chan:(2 * s + 2) * chan, rows], hidden, ((1,), (0,)))
            bias_acc[...] += jnp.sum(grad_pre.astype(F32).reshape(chunk // 8, 8, hidden_units), axis=0)
        return carry

    for turn in range(depth):
        copies = scatter_start(turn)
        lax.fori_loop(chunks * turn // depth, chunks * (turn + 1) // depth, point, 0)
        sums = scatter_sum(turn, copies)
    owned_sums = sums[0]

    columns = plan["columns"]
    rows_each = 2 * chan * columns // size
    wide = hidden_units // columns
    for owner in range(size):
        row = (owner // columns) * rows_each
        source = up_acc if row < chan else down_acc
        row = row % chan
        column = (owner % columns) * wide
        weight_f32[0][owner % first, owner // first] = source[row:row + rows_each, column:column + wide]
    bias_slots[0][digits[-1]] = bias_acc[...]

    weight_copies = weights_start(0)

    left_rows[...] = jnp.zeros_like(left_rows)
    right_rows[...] = jnp.zeros_like(right_rows)
    for s in range(samples):
        coef = owned_sums[:, 2 * s * chan:(2 * s + 1) * chan]
        grad = owned_sums[:, (2 * s + 1) * chan:(2 * s + 2) * chan]
        coef_high = coef.astype(BF16).astype(F32)
        grad_high = grad.astype(BF16).astype(F32)
        left_rows[:, s, :] = coef_high
        left_rows[:, samples + s, :] = coef_high
        left_rows[:, 2 * samples + s, :] = coef - coef_high
        right_rows[:, s, :] = grad_high
        right_rows[:, samples + s, :] = grad - grad_high
        right_rows[:, 2 * samples + s, :] = grad_high
    modes_copy.wait()
    for k in range(owned):
        mixed[k] = dot(right_rows[k].astype(BF16), modes[k], ((1,), (1,)))
    mine = tuple(reversed(digits))
    for s in range(samples):
        value = mixed[:, s, :] + mixed[:, samples + s, :]
        gathered[mine + (slice(None), slice(s * chan, (s + 1) * chan))] = value.astype(BF16)

    per_turn = -(-owned // depth)
    for turn in range(depth):
        coef_copies = gather_start(turn, gathered)
        for k in range(turn * per_turn, min(owned, (turn + 1) * per_turn)):
            outer[k] = dot(left_rows[k].astype(BF16), right_rows[k].astype(BF16), ((0,), (0,)))
        if turn + 1 == depth:
            outer_copy = pltpu.make_async_copy(outer, grad_modes_hbm, out_sems.at[1, 0])
            outer_copy.start()
        weights_sum(turn, weight_copies)
        if turn + 1 < depth:
            weight_copies = weights_start(turn + 1)
        finish(coef_copies)

    def place_of(owner):
        place = []
        for at in range(depth - 1, -1, -1):
            place.append((owner // strides[at]) % radices[at])
        return tuple(place)

    for owner in range(size):
        natural[owner * owned:(owner + 1) * owned, :] = gathered[place_of(owner)]

    def spread(step, carry):
        rows = pl.ds(pl.multiple_of(step * chunk, chunk), chunk)
        value = dot(basis[rows, :], natural[...], ((1,), (0,)))
        for s in range(samples):
            result[s, rows, :] = (value[:, s * chan:(s + 1) * chan] + pointwise[s, rows, :]).astype(BF16)
        pltpu.make_async_copy(result.at[:, rows], grad_input_hbm.at[:, rows], out_sems.at[0, step]).start()
        return carry

    for turn in range(depth):
        weight_copies = gather_start(turn, weights_all)
        lax.fori_loop(chunks * turn // depth, chunks * (turn + 1) // depth, spread, 0)
        finish(weight_copies)

    for owner in range(size):
        row = (owner // columns) * rows_each
        target = grad_up if row < chan else grad_down
        row = row % chan
        column = (owner % columns) * wide
        target[row:row + rows_each, column:column + wide] = weights_all[place_of(owner)]

    for step in range(chunks):
        rows = pl.ds(step * chunk, chunk)
        pltpu.make_async_copy(result.at[:, rows], grad_input_hbm.at[:, rows], out_sems.at[0, step]).wait()
    outer_copy.wait()


def per_device(size, inputs, cotangent, basis, mode_weights, w_up, b_up, w_down):
    samples, here, chan = inputs.shape
    hidden_units = w_up.shape[1]
    total_modes = basis.shape[1]
    owned = total_modes // size
    radices = radices_of(size)
    depth = len(radices)
    chunk = min(512, here)
    load_steps = 4
    columns = max(1, 8 * size // (2 * chan))
    rows_each = 2 * chan * columns // size
    wide = hidden_units // columns
    plan = {
        "size": size, "radices": radices, "chunk": chunk,
        "load_steps": load_steps, "columns": columns,
    }
    width = 2 * samples * chan
    shapes, left = [], size
    for radix in reversed(radices):
        left //= radix
        shapes.append((radix, left))
    rows8 = 8 * (-(-3 * samples // 8))
    backwards = tuple(reversed(radices))
    copies = 4 * sum(radix - 1 for radix in radices)
    vmem = pltpu.VMEM
    scratch = [
        vmem((samples, here, chan), BF16),
        vmem((samples, here, chan), BF16),
        vmem((width, here), BF16),
        vmem((here, total_modes), BF16),
        vmem((owned, chan, chan), BF16),
        vmem((width, total_modes), F32),
        vmem((samples, here, chan), F32),
        vmem((samples, here, chan), BF16),
        vmem((owned, chan, chan), F32),
        vmem((chan, hidden_units), F32),
        vmem((chan, hidden_units), F32),
        vmem((8, hidden_units), F32),
        vmem(backwards + (owned, samples * chan), BF16),
        vmem((total_modes, samples * chan), BF16),
        vmem((owned, rows8, chan), F32),
        vmem((owned, rows8, chan), F32),
        vmem((owned, rows8, chan), F32),
        vmem(backwards + (rows_each, wide), F32),
        pltpu.SemaphoreType.DMA((4, load_steps)),
        pltpu.SemaphoreType.DMA((2, here // chunk)),
        pltpu.SemaphoreType.DMA((copies,)),
        pltpu.SemaphoreType.DMA((copies + sum(radix - 1 for radix in radices),)),
    ]
    copies = 5 * sum(radix - 1 for radix in radices)
    scratch[-2] = pltpu.SemaphoreType.DMA((copies,))
    scratch[-1] = pltpu.SemaphoreType.DMA((copies,))
    scratch += [vmem(shape + (owned, width), F32) for shape in shapes]
    scratch += [vmem(shape + (owned, width), BF16) for shape in shapes]
    scratch += [vmem(shape + (owned, width), BF16) for shape in shapes]
    scratch += [vmem(shape + (rows_each, wide), F32) for shape in shapes]
    scratch += [vmem(shape + (rows_each, wide), F32) for shape in shapes]
    scratch += [vmem((shape[0], 8, hidden_units), F32) for shape in shapes]
    anywhere = pl.BlockSpec(memory_space=pl.ANY)
    inside = pl.BlockSpec(memory_space=pltpu.VMEM)
    grad_input, grad_modes, grad_up, grad_bias, grad_down = pl.pallas_call(
        functools.partial(layer_kernel, plan),
        out_shape=(
            jax.ShapeDtypeStruct((samples, here, chan), BF16),
            jax.ShapeDtypeStruct((owned, chan, chan), F32),
            jax.ShapeDtypeStruct((chan, hidden_units), F32),
            jax.ShapeDtypeStruct((1, hidden_units), F32),
            jax.ShapeDtypeStruct((chan, hidden_units), F32),
        ),
        in_specs=[anywhere] * 4 + [inside] * 3,
        out_specs=(anywhere, anywhere, inside, inside, inside),
        scratch_shapes=scratch,
        compiler_params=pltpu.CompilerParams(
            collective_id=0, has_side_effects=True, vmem_limit_bytes=62 * 1024 * 1024
        ),
        name="layer",
    )(inputs, cotangent, basis, mode_weights, w_up, b_up.reshape(1, hidden_units), w_down)
    return grad_input, grad_modes, grad_up, grad_bias.reshape(hidden_units), grad_down.T


def solution(mesh):
    size = mesh.shape["vert"]
    groups = mesh.shape["samp"]

    def body(*arguments):
        grad_input, grad_modes, grad_up, grad_bias, grad_down = per_device(size, *arguments)
        if groups > 1:
            grad_modes, grad_up, grad_bias, grad_down = lax.psum(
                (grad_modes, grad_up, grad_bias, grad_down), "samp"
            )
        return grad_input, grad_modes, grad_up, grad_bias, grad_down

    in_specs = (
        P("samp", "vert", None),
        P("samp", "vert", None),
        P("vert", None),
        P("vert", None, None),
        P(),
        P(),
        P(),
    )
    out_specs = (P("samp", "vert", None), P("vert", None, None), P(), P(), P())
    return jax.shard_map(body, mesh=mesh, in_specs=in_specs, out_specs=out_specs, check_vma=False)
```

time: 265 us -> 69.4 us (0.26)
  waiting for transfers between devices: 84.9 us -> 0 us
  blocking collectives: 83 us -> 0 us
  matrix products: 61.2 us -> 0 us
  Pallas kernels: 0 us -> 61 us
  local copies, waits for them, and re-layouts: 21.5 us -> 7.59 us
  between operations: 14.1 us -> 0.65 us
    unnamed x2 -> x0, waiting for transfers between devices: 84.9 us -> none
    dot_general x9 -> x0, matrix products: 61.2 us -> none  [the longest x1 14.9 us: pointwise_part(): jnp.dot(flat_cotangent, w_down.T, preferred_element_type=jnp.float32)]
    pallas_call x0 -> x1, Pallas kernels: none -> 61 us  [per_device(): pl.pallas_call(functools.partial(layer_kernel, plan), out_shape=(jax.Shap...]
    psum x1 -> x0, blocking collectives: 41.7 us -> none  [pointwise_part(): sums = lax.psum((local_up, local_bias, local_down), ('samp', 'vert'))]
    all_gather x1 -> x0, blocking collectives: 41.4 us -> none  [spectral_part(): lax.all_gather(grad_coef, 'vert', axis=1, tiled=True)]
    reshape x1 -> x0, local copies, waits for them, and re-layouts: 5.84 us -> none  [pointwise_part(): return (pointwise.reshape(samples_here, vertices_here, channels), sums)]
    unnamed x23 -> x11, local copies, waits for them, and re-layouts: 13.3 us -> 7.59 us
  transfers between devices with their start and end apart: 1 -> 0, of which waited for: 1 -> 0; matrix products, arithmetic and copies ran while one was open for 5% -> 0% of each run, Pallas kernels for 0% -> 0%
where the time goes in v1:
time: 69.4 us; the launch traced here: 69.3 us
  Pallas kernels  61 us (88%)
  local copies, waits for them, and re-layouts  7.59 us (11%)
    pallas_call x1, Pallas kernels, per_device(): pl.pallas_call(functools.partial(layer_kernel, plan), out_shape=(jax.Shap...  61 us
    unnamed x11, local copies, waits for them, and re-layouts  7.59 us

profile of v1, /device:TPU:0, one launch (start us, length us, event | category | flops | bytes accessed | tf_op | source)
XLA Modules:
  0.0 69.3 jit_solution(13873310782787914225)
XLA Ops:
  0.6 61.0 %layer.1 = (bf16[2,4096,128]{2,1,0:T(8,128)(2,1)}, f32[32,128,128]{2,1,0:T(8,128)}, f32[128,512]{1,0:T(8,128)}, f32[1,512]{1,0:T(1,128)}, f32[128,512]{1,0:T(8,128)}) custom-call(bf16[2,4096,128]{2,1,0:T(8,128)(2,1)} %inputs_hbm.1, bf16[2,4096,128]{2,1,0:T(8,128)(2,1)} %cotangent_hbm.1, bf16[4096,1024]{1,0:T(8,128)(2,1)} %basis_hbm.1, ...), custom_call_target="tpu_custom_call" | custom-call | tf_op jit(solution)/shard_map/layer/pallas_call | solution.py:363
  61.7 1.8 %copy.12 = f32[512,128]{1,0:T(8,128)} copy(f32[512,128]{0,1:T(8,128)} %bitcast.3) | data formatting | bytes 524288
  63.5 0.0 copy-start
  63.5 3.2 %copy.17 = bf16[2,4096,128]{2,1,0:T(8,128)(2,1)} copy(bf16[2,4096,128]{2,1,0:T(8,128)(2,1)} %get-tuple-element.25) | data formatting | bytes 4194304
  66.7 0.0 copy-done
  66.7 0.0 copy-start.1
  66.7 0.0 copy-start.2
  66.7 1.3 %copy.18 = f32[32,128,128]{2,1,0:T(8,128)} copy(f32[32,128,128]{2,1,0:T(8,128)S(1)} %copy-done) | data formatting | bytes 4194304
  68.0 0.0 copy-done.1
  68.0 0.7 %copy.19 = f32[128,512]{1,0:T(8,128)} copy(f32[128,512]{1,0:T(8,128)S(1)} %copy-done.1) | data formatting | bytes 524288
  68.7 0.0 copy-done.2
  68.7 0.6 copy.20
Async XLA Ops:
  63.5 3.2 %copy-start = (f32[32,128,128]{2,1,0:T(8,128)S(1)}, f32[32,128,128]{2,1,0:T(8,128)}, u32[]{:S(2)}) copy-start(f32[32,128,128]{2,1,0:T(8,128)} %get-tuple-element.26) | copy-start | bytes 6291460
  66.7 1.3 %copy-start.1 = (f32[128,512]{1,0:T(8,128)S(1)}, f32[128,512]{1,0:T(8,128)}, u32[]{:S(2)}) copy-start(f32[128,512]{1,0:T(8,128)} %get-tuple-element.27) | copy-start | bytes 786436
  66.7 2.0 %copy-start.2 = (f32[1,512]{1,0:T(1,128)S(1)}, f32[1,512]{1,0:T(1,128)}, u32[]{:S(2)}) copy-start(f32[1,512]{1,0:T(1,128)} %get-tuple-element.13) | copy-start | bytes 6148

commit v2 on v1

--- a/solution.py
+++ b/solution.py
@@ -44,12 +44,12 @@
     total_modes = basis.shape[1]
     owned = total_modes // size
     depth = len(radices)
-    coef_f32 = stages[0:depth]
-    coef_send = stages[depth:2 * depth]
-    coef_recv = stages[2 * depth:3 * depth]
-    weight_f32 = stages[3 * depth:4 * depth]
-    weight_recv = stages[4 * depth:5 * depth]
-    bias_slots = stages[5 * depth:6 * depth]
+    orders = plan["orders"]
+    tracks = range(len(orders))
+    kinds = [stages[at * depth:(at + 1) * depth] for at in range(len(stages) // depth)]
+    coef_f32, coef_send, coef_recv = kinds[0:2], kinds[2:4], kinds[4:6]
+    weight_f32, weight_send, weight_recv = kinds[6:8], kinds[8:10], kinds[10:12]
+    bias_slots = kinds[12]
 
     me = lax.axis_index("vert")
     strides = [1] * depth
@@ -102,14 +102,24 @@
 
     lax.fori_loop(0, load_steps, project, 0)
 
-    first = radices[-1]
+    def digits_of(owner, order):
+        return [(owner // strides[at]) % radices[at] for at in order]
+
+    def slot_of(owner, order):
+        found = digits_of(owner, order)
+        rest, scale = 0, 1
+        for at, digit in zip(order[1:], found[1:]):
+            rest += digit * scale
+            scale *= radices[at]
+        return found[0], rest
+
+    half = acc.shape[0] // len(orders)
     for block in range(total_modes // 128):
-        tile = acc[:, block * 128:(block + 1) * 128].T
-        for part in range(128 // owned):
-            owner = block * (128 // owned) + part
-            rows = tile[part * owned:(part + 1) * owned]
-            coef_f32[0][owner % first, owner // first] = rows
-            coef_send[0][owner % first, owner // first] = rows.astype(BF16)
+        for track in tracks:
+            tile = acc[track * half:(track + 1) * half, block * 128:(block + 1) * 128].T
+            for part in range(128 // owned):
+                owner = block * (128 // owned) + part
+                coef_f32[track][0][slot_of(owner, orders[track])] = tile[part * owned:(part + 1) * owned]
 
     pl.semaphore_wait(barrier, peers)
 
@@ -137,59 +147,57 @@
         for copy in copies:
             copy.wait()
 
-    def scatter_start(turn):
-        at = depth - 1 - turn
-        return exchange(at, [(lambda digit: coef_send[turn].at[digit], coef_recv[turn].at[digits[at]])])
-
-    def scatter_sum(turn, copies):
-        at = depth - 1 - turn
+    def scatter_start(turn, held, sent, got):
+        copies = []
+        for track in tracks:
+            at = orders[track][turn]
+            source = (held if turn == 0 else sent)[track][turn]
+            copies += exchange(at, [(lambda digit: source.at[digit], got[track][turn].at[digits[at]])])
+        return copies
+
+    def scatter_sum(turn, copies, held, sent, got, done):
         finish(copies)
-        blocks = coef_f32[turn].shape[1]
-        sums = []
-        for block in range(blocks):
-            value = coef_f32[turn][digits[at], block]
-            for shift in range(1, radices[at]):
-                value = value + coef_recv[turn][peer(at, shift)[0], block].astype(F32)
-            if turn + 1 < depth:
-                radix = radices[at - 1]
-                coef_f32[turn + 1][block % radix, block // radix] = value
-                coef_send[turn + 1][block % radix, block // radix] = value.astype(BF16)
-            else:
-                sums.append(value)
-        return sums
+        for track in tracks:
+            order = orders[track]
+            at = order[turn]
+            for block in range(held[track][turn].shape[1]):
+                value = held[track][turn][digits[at], block]
+                for shift in range(1, radices[at]):
+                    value = value + got[track][turn][peer(at, shift)[0], block].astype(F32)
+                if turn + 1 < depth:
+                    radix = radices[order[turn + 1]]
+                    held[track][turn + 1][block % radix, block // radix] = value
+                    sent[track][turn + 1][block % radix, block // radix] = value.astype(BF16)
+                else:
+                    done(track, value)
+
+    mine = [tuple(digits[at] for at in order) for order in orders]
+
+    def keep_weights(track, value):
+        weights_all[(track,) + mine[track]] = value.astype(BF16)
 
     def weights_start(turn):
-        at = depth - 1 - turn
-        pairs = [
-            (lambda digit: weight_f32[turn].at[digit], weight_recv[turn].at[digits[at]]),
-            (lambda digit: bias_slots[turn].at[digits[at]], bias_slots[turn].at[digits[at]]),
-        ]
-        return exchange(at, pairs)
+        at = orders[0][turn]
+        slot = bias_slots[turn].at[digits[at]]
+        return scatter_start(turn, weight_f32, weight_send, weight_recv) + exchange(at, [(lambda digit: slot, slot)])
 
     def weights_sum(turn, copies):
-        at = depth - 1 - turn
-        finish(copies)
-        blocks = weight_f32[turn].shape[1]
-        for block in range(blocks):
-            value = weight_f32[turn][digits[at], block]
-            for shift in range(1, radices[at]):
-                value = value + weight_recv[turn][peer(at, shift)[0], block]
-            if turn + 1 < depth:
-                radix = radices[at - 1]
-                weight_f32[turn + 1][block % radix, block // radix] = value
-            else:
-                weights_all[tuple(reversed(digits))] = value
+        scatter_sum(turn, copies, weight_f32, weight_send, weight_recv, keep_weights)
         bias = bias_slots[turn][0]
-        for slot in range(1, radices[at]):
+        for slot in range(1, radices[orders[0][turn]]):
             bias = bias + bias_slots[turn][slot]
         if turn + 1 < depth:
-            bias_slots[turn + 1][digits[at - 1]] = bias
+            bias_slots[turn + 1][digits[orders[0][turn + 1]]] = bias
         else:
             grad_bias[...] = jnp.sum(bias, axis=0, keepdims=True)
 
     def gather_start(turn, ref):
-        held = ref.at[tuple(reversed(digits[turn:]))]
-        return exchange(turn, [(lambda digit: held, held)])
+        copies = []
+        for track in tracks:
+            order = orders[track]
+            held = ref.at[(track,) + mine[track][:depth - turn]]
+            copies += exchange(order[depth - 1 - turn], [(lambda digit: held, held)])
+        return copies
 
     chunk = plan["chunk"]
     chunks = here // chunk
@@ -200,10 +208,10 @@
             z = dot(xs[s, rows, :], w_up[...], ((1,), (0,))) + b_up[...]
             square = z * z
             t = jnp.tanh(z * (ROOT + (ROOT * CUBE) * square))
-            half = 0.5 * z
+            middle = 0.5 * z
             plus = 1.0 + t
-            hidden = (half * plus).astype(BF16)
-            slope = plus * (0.5 + half * (1.0 - t) * (ROOT + (3.0 * ROOT * CUBE) * square))
+            hidden = (middle * plus).astype(BF16)
+            slope = plus * (0.5 + middle * (1.0 - t) * (ROOT + (3.0 * ROOT * CUBE) * square))
             grad_hidden = dot(cs[s, rows, :], w_down[...], ((1,), (1,)))
             grad_pre = (grad_hidden * slope).astype(BF16)
             pointwise[s, rows, :] = dot(grad_pre, w_up[...], ((1,), (1,)))
@@ -212,22 +220,26 @@
             bias_acc[...] += jnp.sum(grad_pre.astype(F32).reshape(chunk // 8, 8, hidden_units), axis=0)
         return carry
 
+    totals = []
     for turn in range(depth):
-        copies = scatter_start(turn)
+        copies = scatter_start(turn, coef_f32, coef_send, coef_recv)
         lax.fori_loop(chunks * turn // depth, chunks * (turn + 1) // depth, point, 0)
-        sums = scatter_sum(turn, copies)
-    owned_sums = sums[0]
+        scatter_sum(turn, copies, coef_f32, coef_send, coef_recv, lambda track, value: totals.append(value))
+    owned_sums = jnp.concatenate(totals, axis=1)
 
     columns = plan["columns"]
     rows_each = 2 * chan * columns // size
     wide = hidden_units // columns
+    part_wide = wide // len(orders)
     for owner in range(size):
         row = (owner // columns) * rows_each
         source = up_acc if row < chan else down_acc
         row = row % chan
         column = (owner % columns) * wide
-        weight_f32[0][owner % first, owner // first] = source[row:row + rows_each, column:column + wide]
-    bias_slots[0][digits[-1]] = bias_acc[...]
+        for track in tracks:
+            start = column + track * part_wide
+            weight_f32[track][0][slot_of(owner, orders[track])] = source[row:row + rows_each, start:start + part_wide]
+    bias_slots[0][digits[orders[0][0]]] = bias_acc[...]
 
     weight_copies = weights_start(0)
 
@@ -247,10 +259,10 @@
     modes_copy.wait()
     for k in range(owned):
         mixed[k] = dot(right_rows[k].astype(BF16), modes[k], ((1,), (1,)))
-    mine = tuple(reversed(digits))
-    for s in range(samples):
-        value = mixed[:, s, :] + mixed[:, samples + s, :]
-        gathered[mine + (slice(None), slice(s * chan, (s + 1) * chan))] = value.astype(BF16)
+    value = jnp.concatenate([mixed[:, s, :] + mixed[:, samples + s, :] for s in range(samples)], axis=1)
+    part_chan = samples * chan // len(orders)
+    for track in tracks:
+        gathered[(track,) + mine[track]] = value[:, track * part_chan:(track + 1) * part_chan].astype(BF16)
 
     per_turn = -(-owned // depth)
     for turn in range(depth):
@@ -265,14 +277,10 @@
             weight_copies = weights_start(turn + 1)
         finish(coef_copies)
 
-    def place_of(owner):
-        place = []
-        for at in range(depth - 1, -1, -1):
-            place.append((owner // strides[at]) % radices[at])
-        return tuple(place)
-
     for owner in range(size):
-        natural[owner * owned:(owner + 1) * owned, :] = gathered[place_of(owner)]
+        for track in tracks:
+            natural[owner * owned:(owner + 1) * owned, track * part_chan:(track + 1) * part_chan] = gathered[
+                (track,) + tuple(digits_of(owner, orders[track]))]
 
     def spread(step, carry):
         rows = pl.ds(pl.multiple_of(step * chunk, chunk), chunk)
@@ -292,12 +300,46 @@
         target = grad_up if row < chan else grad_down
         row = row % chan
         column = (owner % columns) * wide
-        target[row:row + rows_each, column:column + wide] = weights_all[place_of(owner)]
+        for track in tracks:
+            start = column + track * part_wide
+            target[row:row + rows_each, start:start + part_wide] = weights_all[
+                (track,) + tuple(digits_of(owner, orders[track]))].astype(F32)
 
     for step in range(chunks):
         rows = pl.ds(step * chunk, chunk)
         pltpu.make_async_copy(result.at[:, rows], grad_input_hbm.at[:, rows], out_sems.at[0, step]).wait()
     outer_copy.wait()
+
+
+def place_kernel(
+    steps, input_from, modes_from, up_from, bias_from, down_from,
+    input_to, modes_to, up_to, bias_to, down_to, input_held, modes_held, sems,
+):
+    def parts(step):
+        rows = input_held.shape[1] // steps
+        here = pl.ds(step * rows, rows)
+        kept = modes_held.shape[0] // steps
+        modes = pl.ds(step * kept, kept)
+        return (
+            (input_from.at[:, here], input_held.at[:, here], input_to.at[:, here]),
+            (modes_from.at[modes], modes_held.at[modes], modes_to.at[modes]),
+        )
+
+    reads, writes = [], []
+    for step in range(steps):
+        for kind, (source, held, target) in enumerate(parts(step)):
+            reads.append(pltpu.make_async_copy(source, held, sems.at[kind, step]))
+            writes.append(pltpu.make_async_copy(held, target, sems.at[2 + kind, step]))
+    for copy in reads:
+        copy.start()
+    up_to[...] = up_from[...]
+    bias_to[...] = bias_from[...]
+    down_to[...] = down_from[...].T
+    for read, write in zip(reads, writes):
+        read.wait()
+        write.start()
+    for write in writes:
+        write.wait()
 
 
 def per_device(size, inputs, cotangent, basis, mode_weights, w_up, b_up, w_down):
@@ -309,7 +351,7 @@
     depth = len(radices)
     chunk = min(512, here)
     load_steps = 4
-    columns = max(1, 8 * size // (2 * chan))
+    columns = max(1, min(16 * size // (2 * chan), hidden_units // 256))
     rows_each = 2 * chan * columns // size
     wide = hidden_units // columns
     plan = {
@@ -317,13 +359,24 @@
         "load_steps": load_steps, "columns": columns,
     }
     width = 2 * samples * chan
-    shapes, left = [], size
-    for radix in reversed(radices):
-        left //= radix
-        shapes.append((radix, left))
+    straight = list(reversed(range(depth)))
+    crossed = list(straight)
+    if depth > 2:
+        crossed[1], crossed[2] = crossed[2], crossed[1]
+    orders = (tuple(straight), tuple(crossed))
+    plan["orders"] = orders
+    shapes = []
+    for order in orders:
+        left, found = size, []
+        for at in order:
+            left //= radices[at]
+            found.append((radices[at], left))
+        shapes.append(found)
     rows8 = 8 * (-(-3 * samples // 8))
-    backwards = tuple(reversed(radices))
-    copies = 4 * sum(radix - 1 for radix in radices)
+    backwards = tuple(radices[at] for at in orders[0])
+    other = tuple(radices[at] for at in orders[1])
+    assert backwards == other
+    copies = 9 * sum(radix - 1 for radix in radices)
     vmem = pltpu.VMEM
     scratch = [
         vmem((samples, here, chan), BF16),
@@ -338,26 +391,29 @@
         vmem((chan, hidden_units), F32),
         vmem((chan, hidden_units), F32),
         vmem((8, hidden_units), F32),
-        vmem(backwards + (owned, samples * chan), BF16),
+        vmem((2,) + backwards + (owned, samples * chan // 2), BF16),
         vmem((total_modes, samples * chan), BF16),
         vmem((owned, rows8, chan), F32),
         vmem((owned, rows8, chan), F32),
         vmem((owned, rows8, chan), F32),
-        vmem(backwards + (rows_each, wide), F32),
+        vmem((2,) + backwards + (rows_each, wide // 2), BF16),
         pltpu.SemaphoreType.DMA((4, load_steps)),
         pltpu.SemaphoreType.DMA((2, here // chunk)),
         pltpu.SemaphoreType.DMA((copies,)),
-        pltpu.SemaphoreType.DMA((copies + sum(radix - 1 for radix in radices),)),
+        pltpu.SemaphoreType.DMA((copies,)),
     ]
-    copies = 5 * sum(radix - 1 for radix in radices)
-    scratch[-2] = pltpu.SemaphoreType.DMA((copies,))
-    scratch[-1] = pltpu.SemaphoreType.DMA((copies,))
-    scratch += [vmem(shape + (owned, width), F32) for shape in shapes]
-    scratch += [vmem(shape + (owned, width), BF16) for shape in shapes]
-    scratch += [vmem(shape + (owned, width), BF16) for shape in shapes]
-    scratch += [vmem(shape + (rows_each, wide), F32) for shape in shapes]
-    scratch += [vmem(shape + (rows_each, wide), F32) for shape in shapes]
-    scratch += [vmem((shape[0], 8, hidden_units), F32) for shape in shapes]
+
+    def stage_buffers(tail, first_type, later_type):
+        return [
+            vmem(shape + tail, later_type if turn else first_type)
+            for found in shapes for turn, shape in enumerate(found)
+        ]
+
+    for tail in ((owned, width // 2), (rows_each, wide // 2)):
+        scratch += stage_buffers(tail, F32, F32)
+        scratch += stage_buffers(tail, BF16, BF16)
+        scratch += stage_buffers(tail, F32, BF16)
+    scratch += [vmem((shape[0], 8, hidden_units), F32) for shape in shapes[0]]
     anywhere = pl.BlockSpec(memory_space=pl.ANY)
     inside = pl.BlockSpec(memory_space=pltpu.VMEM)
     grad_input, grad_modes, grad_up, grad_bias, grad_down = pl.pallas_call(
@@ -377,7 +433,27 @@
         ),
         name="layer",
     )(inputs, cotangent, basis, mode_weights, w_up, b_up.reshape(1, hidden_units), w_down)
-    return grad_input, grad_modes, grad_up, grad_bias.reshape(hidden_units), grad_down.T
+    steps = 4
+    grad_input, grad_modes, grad_up, grad_bias, grad_down = pl.pallas_call(
+        functools.partial(place_kernel, steps),
+        out_shape=(
+            jax.ShapeDtypeStruct((samples, here, chan), BF16),
+            jax.ShapeDtypeStruct((owned, chan, chan), F32),
+            jax.ShapeDtypeStruct((chan, hidden_units), F32),
+            jax.ShapeDtypeStruct((1, hidden_units), F32),
+            jax.ShapeDtypeStruct((hidden_units, chan), F32),
+        ),
+        in_specs=[anywhere] * 2 + [inside] * 3,
+        out_specs=(anywhere, anywhere, inside, inside, inside),
+        scratch_shapes=[
+            vmem((samples, here, chan), BF16),
+            vmem((owned, chan, chan), F32),
+            pltpu.SemaphoreType.DMA((4, steps)),
+        ],
+        compiler_params=pltpu.CompilerParams(vmem_limit_bytes=16 * 1024 * 1024),
+        name="place",
+    )(grad_input, grad_modes, grad_up, grad_bias, grad_down)
+    return grad_input, grad_modes, grad_up, grad_bias.reshape(hidden_units), grad_down
 
 
 def solution(mesh):

time: 69.4 us -> 66.3 us (0.955)
  local copies, waits for them, and re-layouts: 7.59 us -> 5.74 us
  Pallas kernels: 61 us -> 59.6 us
    pallas_call x1, Pallas kernels: 61 us -> 56.3 us  [per_device(): pl.pallas_call(functools.partial(layer_kernel, plan), out_shape=(jax.Shap...]
    pallas_call x0 -> x1, Pallas kernels: none -> 3.35 us  [per_device(): pl.pallas_call(functools.partial(place_kernel, steps), out_shape=(jax.Sha...]
    unnamed x11 -> x10, local copies, waits for them, and re-layouts: 7.59 us -> 5.74 us
where the time goes in v2:
time: 66.3 us; the launch traced here: 66 us
  Pallas kernels  59.6 us (90%)
  local copies, waits for them, and re-layouts  5.74 us (9%)
    pallas_call x1, Pallas kernels, per_device(): pl.pallas_call(functools.partial(layer_kernel, plan), out_shape=(jax.Shap...  56.3 us
    unnamed x10, local copies, waits for them, and re-layouts  5.74 us
    pallas_call x1, Pallas kernels, per_device(): pl.pallas_call(functools.partial(place_kernel, steps), out_shape=(jax.Sha...  3.35 us

profile of v2, /device:TPU:0, one launch (start us, length us, event | category | flops | bytes accessed | tf_op | source)
XLA Modules:
  0.0 66.0 jit_solution(5803103709786280755)
XLA Ops:
  0.6 56.3 %layer.1 = (bf16[2,4096,128]{2,1,0:T(8,128)(2,1)}, f32[32,128,128]{2,1,0:T(8,128)}, f32[128,512]{1,0:T(8,128)}, f32[1,512]{1,0:T(1,128)}, f32[128,512]{1,0:T(8,128)}) custom-call(bf16[2,4096,128]{2,1,0:T(8,128)(2,1)} %inputs_hbm.1, bf16[2,4096,128]{2,1,0:T(8,128)(2,1)} %cotangent_hbm.1, bf16[4096,1024]{1,0:T(8,128)(2,1)} %basis_hbm.1, ...), custom_call_target="tpu_custom_call" | custom-call | tf_op jit(solution)/shard_map/layer/pallas_call | solution.py:419
  56.9 0.0 copy-start
  56.9 1.6 %copy-done = bf16[2,4096,128]{2,1,0:T(8,128)(2,1)S(1)} copy-done((bf16[2,4096,128]{2,1,0:T(8,128)(2,1)S(1)}, bf16[2,4096,128]{2,1,0:T(8,128)(2,1)}, u32[]{:S(2)}) %copy-start) | copy-done | bytes 2097176
  58.5 0.0 copy-start.1
  58.5 1.6 %copy-done.1 = f32[32,128,128]{2,1,0:T(8,128)S(1)} copy-done((f32[32,128,128]{2,1,0:T(8,128)S(1)}, f32[32,128,128]{2,1,0:T(8,128)}, u32[]{:S(2)}) %copy-start.1) | copy-done | bytes 2097176
  60.1 0.0 copy-start.2
  60.1 0.9 %copy-done.2 = f32[128,512]{1,0:T(8,128)S(1)} copy-done((f32[128,512]{1,0:T(8,128)S(1)}, f32[128,512]{1,0:T(8,128)}, u32[]{:S(2)}) %copy-start.2) | copy-done | bytes 262168
  61.1 0.0 copy-start.3
  61.1 0.9 %copy-done.3 = f32[128,512]{1,0:T(8,128)S(1)} copy-done((f32[128,512]{1,0:T(8,128)S(1)}, f32[128,512]{1,0:T(8,128)}, u32[]{:S(2)}) %copy-start.3) | copy-done | bytes 262168
  62.0 0.0 copy-start.4
  62.0 0.7 %copy-done.4 = f32[1,512]{1,0:T(1,128)S(1)} copy-done((f32[1,512]{1,0:T(1,128)S(1)}, f32[1,512]{1,0:T(1,128)}, u32[]{:S(2)}) %copy-start.4) | copy-done | bytes 2072
  62.7 3.4 %place.1 = (bf16[2,4096,128]{2,1,0:T(8,128)(2,1)}, f32[32,128,128]{2,1,0:T(8,128)}, f32[128,512]{1,0:T(8,128)}, f32[1,512]{1,0:T(1,128)}, f32[512,128]{1,0:T(8,128)}) custom-call(bf16[2,4096,128]{2,1,0:T(8,128)(2,1)S(1)} %copy-done, f32[32,128,128]{2,1,0:T(8,128)S(1)} %copy-done.1, f32[128,512]{1,0:T(8,128)S(1)} %copy-done.2, f32[1,512]{1,0:T(1,128)S(1)} %copy-done.4, ...), custom_call_target="tpu_custom_call" | custom-call | tf_op jit(solution)/shard_map/place/pallas_call | solution.py:437
Async XLA Ops:
  56.9 1.6 %copy-start = (bf16[2,4096,128]{2,1,0:T(8,128)(2,1)S(1)}, bf16[2,4096,128]{2,1,0:T(8,128)(2,1)}, u32[]{:S(2)}) copy-start(bf16[2,4096,128]{2,1,0:T(8,128)(2,1)} %get-tuple-element.15.input_from) | copy-start | bytes 6291460
  58.5 1.6 %copy-start.1 = (f32[32,128,128]{2,1,0:T(8,128)S(1)}, f32[32,128,128]{2,1,0:T(8,128)}, u32[]{:S(2)}) copy-start(f32[32,128,128]{2,1,0:T(8,128)} %get-tuple-element.16.modes_from) | copy-start | bytes 6291460
  60.1 0.9 %copy-start.2 = (f32[128,512]{1,0:T(8,128)S(1)}, f32[128,512]{1,0:T(8,128)}, u32[]{:S(2)}) copy-start(f32[128,512]{1,0:T(8,128)} %get-tuple-element.17.up_from) | copy-start | bytes 786436
  61.1 0.9 %copy-start.3 = (f32[128,512]{1,0:T(8,128)S(1)}, f32[128,512]{1,0:T(8,128)}, u32[]{:S(2)}) copy-start(f32[128,512]{1,0:T(8,128)} %get-tuple-element.19.down_from) | copy-start | bytes 786436
  62.0 0.7 %copy-start.4 = (f32[1,512]{1,0:T(1,128)S(1)}, f32[1,512]{1,0:T(1,128)}, u32[]{:S(2)}) copy-start(f32[1,512]{1,0:T(1,128)} %get-tuple-element.18.bias_from) | copy-start | bytes 6148

commit v3 on v2

--- a/solution.py
+++ b/solution.py
@@ -450,7 +450,7 @@
             vmem((owned, chan, chan), F32),
             pltpu.SemaphoreType.DMA((4, steps)),
         ],
-        compiler_params=pltpu.CompilerParams(vmem_limit_bytes=16 * 1024 * 1024),
+        compiler_params=pltpu.CompilerParams(vmem_limit_bytes=62 * 1024 * 1024),
         name="place",
     )(grad_input, grad_modes, grad_up, grad_bias, grad_down)
     return grad_input, grad_modes, grad_up, grad_bias.reshape(hidden_units), grad_down

time: 66.3 us -> 62.5 us (0.943)
  local copies, waits for them, and re-layouts: 5.74 us -> 0 us
  Pallas kernels: 59.6 us -> 61.7 us
    unnamed x10 -> x0, local copies, waits for them, and re-layouts: 5.74 us -> none
    pallas_call x1, Pallas kernels: 3.35 us -> 5.4 us  [per_device(): pl.pallas_call(functools.partial(place_kernel, steps), out_shape=(jax.Sha...]
where the time goes in v3:
time: 62.5 us; the launch traced here: 62.3 us
  Pallas kernels  61.7 us (99%)
  between operations  0.64 us (1%)
    pallas_call x1, Pallas kernels, per_device(): pl.pallas_call(functools.partial(layer_kernel, plan), out_shape=(jax.Shap...  56.2 us
    pallas_call x1, Pallas kernels, per_device(): pl.pallas_call(functools.partial(place_kernel, steps), out_shape=(jax.Sha...  5.4 us

profile of v3, /device:TPU:0, one launch (start us, length us, event | category | flops | bytes accessed | tf_op | source)
XLA Modules:
  0.0 62.3 jit_solution(8829487603135192992)
XLA Ops:
  0.6 56.2 %layer.1 = (bf16[2,4096,128]{2,1,0:T(8,128)(2,1)}, f32[32,128,128]{2,1,0:T(8,128)}, f32[128,512]{1,0:T(8,128)}, f32[1,512]{1,0:T(1,128)}, f32[128,512]{1,0:T(8,128)}) custom-call(bf16[2,4096,128]{2,1,0:T(8,128)(2,1)} %inputs_hbm.1, bf16[2,4096,128]{2,1,0:T(8,128)(2,1)} %cotangent_hbm.1, bf16[4096,1024]{1,0:T(8,128)(2,1)} %basis_hbm.1, ...), custom_call_target="tpu_custom_call" | custom-call | tf_op jit(solution)/shard_map/layer/pallas_call | solution.py:419
  56.9 5.4 %place.1 = (bf16[2,4096,128]{2,1,0:T(8,128)(2,1)}, f32[32,128,128]{2,1,0:T(8,128)}, f32[128,512]{1,0:T(8,128)}, f32[1,512]{1,0:T(1,128)}, f32[512,128]{1,0:T(8,128)}) custom-call(bf16[2,4096,128]{2,1,0:T(8,128)(2,1)} %get-tuple-element.15.input_from, f32[32,128,128]{2,1,0:T(8,128)} %get-tuple-element.16.modes_from, f32[128,512]{1,0:T(8,128)} %get-tuple-element.17.up_from, ...), custom_call_target="tpu_custom_call" | custom-call | tf_op jit(solution)/shard_map/place/pallas_call | solution.py:437
